TPU v7x, 32 devices: a whole 2x2x4 slice. The times are simulated.
32 devices in a mesh: seq: 2 (over y), rows: 16 (over z, x, core).
Axes of the slice: x: 2, y: 2, z: 4, core: 2. Of those that a mesh axis runs over, the one named last changes fastest.
Arguments:
- hidden: bfloat16 [16, 1024, 384], P('rows', 'seq'), may hold values from -6 to 6
- grad_out: bfloat16 [16, 1024, 384], P('rows', 'seq'), may hold values from -6 to 6
- grad_mask: int32 [16, 1024], P('rows', 'seq'), may hold values from 0 to 1, as said below
- w_query: bfloat16 [384, 384], replicated, may hold values from -0.4375 to 0.4375
- w_key: bfloat16 [384, 384], replicated, may hold values from -0.4375 to 0.4375
- w_value: bfloat16 [384, 384], replicated, may hold values from -0.3125 to 0.3125
- w_output: bfloat16 [384, 384], replicated, may hold values from -1.25 to 1.25
- rel_table: bfloat16 [512, 384], replicated, may hold values from -6 to 6
- w_pos_key: bfloat16 [384, 384], replicated, may hold values from -0.4375 to 0.4375
- w_pos_query: bfloat16 [384, 384], replicated, may hold values from -0.4375 to 0.4375
- attn_biases: bfloat16 [4, 384], replicated, may hold values from -1.796875 to 1.796875
- norm_gains: bfloat16 [2, 384], replicated, may hold values from 0.25 to 1.75
- norm_shifts: bfloat16 [2, 384], replicated, may hold values from -1.796875 to 1.796875
- w_inner: bfloat16 [384, 1536], replicated, may hold values from -0.3125 to 0.3125
- inner_bias: bfloat16 [1536], replicated, may hold values from -1.796875 to 1.796875
- w_outer: bfloat16 [1536, 384], replicated, may hold values from -0.15625 to 0.15625
- outer_bias: bfloat16 [384], replicated, may hold values from -1.796875 to 1.796875
Outputs:
- result: bfloat16 [16, 1024, 384], P('rows', 'seq')
- grad_hidden: bfloat16 [16, 1024, 384], P('rows', 'seq')
- grad_w_query: float32 [384, 384], P('rows')
- grad_w_key: float32 [384, 384], P('rows')
- grad_w_value: float32 [384, 384], P('rows')
- grad_w_output: float32 [384, 384], P('rows')
- grad_rel_table: float32 [512, 384], P(None, 'rows')
- grad_w_pos_key: float32 [384, 384], P('rows')
- grad_w_pos_query: float32 [384, 384], P('rows')
- grad_attn_biases: float32 [4, 384], P(None, 'rows')
- grad_norm_gains: float32 [2, 384], P(None, 'rows')
- grad_norm_shifts: float32 [2, 384], P(None, 'rows')
- grad_w_inner: float32 [384, 1536], P('rows')
- grad_inner_bias: float32 [1536], replicated
- grad_w_outer: float32 [1536, 384], P(None, 'rows')
- grad_outer_bias: float32 [384], P('rows')
Inputs may be any that keep to these rules, and one draw needn't show every extreme that they name: `grad_mask`: in every sequence a share of the positions is 1, taken as 1024 * p // 100 positions where the sequences' p run evenly from 5 to 40 over the 16 sequences in an order drawn from the seed; the marked positions are spread at random.
All inputs are finite; a program needn't handle non-finite values.
Results may differ from a plain program's by a relative error of at most 0.02.
Values may be sent and summed in bfloat16 or wider, within the bound.
No kernel may reach another device: no remote copies, remote signals or barrier semaphores. Data moves between devices by JAX's collectives and lax.ppermute only.
A program may use at most 128 MiB of HBM per device.

v0:
```python
from functools import partial
import math

import jax
import jax.numpy as jnp
from jax import lax
from jax.sharding import PartitionSpec as P

HEADS = 6


norm_eps = 1e-07
masked_score = -1e30
highest = lax.Precision.HIGHEST


def extended(block, sides, width):
    for axis, dim in sides:
        count = lax.axis_size(axis)
        forward = [(i, i + 1) for i in range(count - 1)]
        backward = [(target, source) for source, target in forward]
        low = lax.ppermute(
            lax.slice_in_dim(block, block.shape[dim] - width, None, axis=dim), axis, forward
        )
        high = lax.ppermute(lax.slice_in_dim(block, 0, width, axis=dim), axis, backward)
        block = jnp.concatenate([low, block, high], axis=dim)
    return block


def shifted(value, axis, steps):
    count = lax.axis_size(axis)
    initial, last = (max(0, -steps), min(count, count - steps))
    return lax.ppermute(value, axis, [(source, source + steps) for source in range(initial, last)])


def layer_norm(values, gain, shift):
    centre = values - jnp.mean(values, axis=-1, keepdims=True)
    spread = jnp.mean(centre * centre, axis=-1, keepdims=True)
    return centre * lax.rsqrt(spread + norm_eps) * gain + shift


def exact_gelu(values):
    return jax.nn.gelu(values, approximate=False)


def to_band(matrix, columns):
    height, length = matrix.shape
    flat = jnp.pad(matrix.reshape(height * length), (0, height + 1))
    flat = flat[1 : 1 + height * (length + 1)]
    return flat.reshape(height, length + 1)[:, :columns]


def from_band(band, length):
    height, columns = band.shape
    padded = jnp.pad(band, ((0, 0), (0, length + 1 - columns)))
    flat = jnp.pad(padded.reshape(height * (length + 1)), (1, 0))
    return flat[: height * length].reshape(height, length)


def raw_scores(query, window_keys, keys_reversed, queries_shifted):
    direct = jnp.einsum("id,jd->ij", query, window_keys, preferred_element_type=jnp.float32)
    content = to_band(direct, keys_reversed.shape[0])
    to_pos = jnp.einsum("id,td->it", query, keys_reversed, preferred_element_type=jnp.float32)
    from_pos = jnp.einsum(
        "jd,td->tj", window_keys, queries_shifted, preferred_element_type=jnp.float32
    )
    return content + to_pos + to_band(from_pos, query.shape[0]).T


def attend_head(item, valid, scale):
    query, window_keys, window_values, keys_reversed, queries_shifted = item
    scores = jnp.where(
        valid, raw_scores(query, window_keys, keys_reversed, queries_shifted) * scale, masked_score
    )
    largest = jnp.max(scores, axis=1, keepdims=True)
    weights = jnp.exp(scores - largest)
    totals = jnp.sum(weights, axis=1, keepdims=True)
    probs_low = from_band((weights / totals).astype(jnp.bfloat16), window_keys.shape[0])
    context = jnp.einsum("ij,jd->id", probs_low, window_values, preferred_element_type=jnp.float32)
    return (context, (largest + jnp.log(totals))[:, 0])


def attend_back(item, valid, scale):
    query, window_keys, window_values, keys_reversed, queries_shifted, d_context, log_total = item
    length = window_keys.shape[0]
    scores = jnp.where(
        valid, raw_scores(query, window_keys, keys_reversed, queries_shifted) * scale, masked_score
    )
    probs = jnp.exp(scores - log_total[:, None])
    probs_low = from_band(probs.astype(jnp.bfloat16), length)
    d_full = jnp.einsum("id,jd->ij", d_context, window_values, preferred_element_type=jnp.float32)
    d_probs = to_band(d_full, keys_reversed.shape[0])
    d_values = jnp.einsum("ij,id->jd", probs_low, d_context, preferred_element_type=jnp.float32)
    d_scores = probs * (d_probs - jnp.sum(probs * d_probs, axis=1, keepdims=True))
    d_raw = (d_scores * scale).astype(jnp.bfloat16)
    d_direct = from_band(d_raw, length)
    d_shifted = from_band(d_raw.T, length)
    d_query = jnp.einsum("ij,jd->id", d_direct, window_keys, preferred_element_type=jnp.float32)
    d_query = d_query + jnp.einsum(
        "it,td->id", d_raw, keys_reversed, preferred_element_type=jnp.float32
    )
    d_keys = jnp.einsum("ij,id->jd", d_direct, query, preferred_element_type=jnp.float32)
    d_keys = d_keys + jnp.einsum(
        "tj,td->jd", d_shifted, queries_shifted, preferred_element_type=jnp.float32
    )
    d_reversed = jnp.einsum("it,id->td", d_raw, query, preferred_element_type=jnp.float32)
    d_pos_shifted = jnp.einsum(
        "tj,jd->td", d_shifted, window_keys, preferred_element_type=jnp.float32
    )
    return (d_query, d_keys, d_values, d_reversed, d_pos_shifted)


def local(
    hidden,
    grad_out,
    grad_mask,
    w_query,
    w_key,
    w_value,
    w_output,
    rel_table,
    w_pos_key,
    w_pos_query,
    attn_biases,
    norm_gains,
    norm_shifts,
    w_inner,
    inner_bias,
    w_outer,
    outer_bias,
):
    count, block, width = hidden.shape
    heads = HEADS
    head = width // heads
    span = rel_table.shape[0] // 2
    window = block + 2 * span
    scale = 1.0 / math.sqrt(3.0 * head)
    tokens = count * block
    flat_in = hidden.reshape(tokens, width)
    biases = attn_biases.astype(jnp.float32)
    gains = norm_gains.astype(jnp.float32)
    shifts = norm_shifts.astype(jnp.float32)

    def project(left, right):
        return jnp.dot(left, right, preferred_element_type=jnp.float32)

    def by_head(matrix, rows):
        return (
            matrix.reshape(count, rows, heads, head)
            .transpose(0, 2, 1, 3)
            .reshape(count * heads, rows, head)
        )

    def from_heads(stack, rows):
        return (
            stack.reshape(count, heads, rows, head)
            .transpose(0, 2, 1, 3)
            .reshape(count * rows, width)
        )

    def per_head_table(table):
        split = table.reshape(2 * span, heads, head).transpose(1, 0, 2)
        return split[None].reshape(count * heads, 2 * span, head)

    def table_sum(stack):
        return (
            stack.reshape(count, heads, 2 * span, head)
            .sum(axis=0)
            .transpose(1, 0, 2)
            .reshape(2 * span, width)
        )

    query = (project(flat_in, w_query) + biases[0]).astype(jnp.bfloat16)
    keys = project(flat_in, w_key).astype(jnp.bfloat16)
    values = (project(flat_in, w_value) + biases[1]).astype(jnp.bfloat16)
    pos_keys = project(rel_table, w_pos_key).astype(jnp.bfloat16)
    pos_queries = (project(rel_table, w_pos_query) + biases[2]).astype(jnp.bfloat16)
    pairs = jnp.concatenate([keys, values], axis=1).reshape(count, block, 2 * width)
    framed = extended(pairs, (("seq", 1),), span)
    first = lax.axis_index("seq") * block
    length = block * lax.axis_size("seq")
    row_place = jnp.arange(block, dtype=jnp.int32)[:, None]
    band_place = jnp.arange(2 * span, dtype=jnp.int32)[None, :]
    target = first + row_place + 1 + band_place - span
    valid = (target >= 0) & (target < length)
    head_query = by_head(query, block)
    head_keys = by_head(framed[:, :, :width].reshape(count * window, width), window)
    head_values = by_head(framed[:, :, width:].reshape(count * window, width), window)
    head_reversed = per_head_table(pos_keys[::-1])
    head_shifted = per_head_table(jnp.concatenate([pos_queries[1:], pos_queries[-1:]], axis=0))
    items = (head_query, head_keys, head_values, head_reversed, head_shifted)
    context_heads, log_total = lax.map(partial(attend_head, valid=valid, scale=scale), items)
    context_low = from_heads(context_heads, block).astype(jnp.bfloat16)
    attended = project(context_low, w_output) + biases[3]
    first_sum = flat_in.astype(jnp.float32) + attended
    normed, first_back = jax.vjp(layer_norm, first_sum, gains[0], shifts[0])
    normed_low = normed.astype(jnp.bfloat16)
    inner = project(normed_low, w_inner) + inner_bias.astype(jnp.float32)
    active, gelu_back = jax.vjp(exact_gelu, inner)
    active_low = active.astype(jnp.bfloat16)
    outer = project(active_low, w_outer) + outer_bias.astype(jnp.float32)
    output_full, second_back = jax.vjp(layer_norm, normed + outer, gains[1], shifts[1])
    result = output_full.astype(jnp.bfloat16).reshape(count, block, width)
    cotangent = grad_out.reshape(tokens, width).astype(jnp.float32) * grad_mask.reshape(tokens)[
        :, None
    ].astype(jnp.float32)
    d_second, d_gain_two, d_shift_two = second_back(cotangent)
    d_outer = d_second.astype(jnp.bfloat16)
    grad_w_outer = jnp.einsum("tf,td->fd", active_low, d_outer, preferred_element_type=jnp.float32)
    grad_outer_bias = jnp.sum(d_outer.astype(jnp.float32), axis=0)
    (d_active,) = gelu_back(
        jnp.einsum("td,fd->tf", d_outer, w_outer, preferred_element_type=jnp.float32)
    )
    d_inner = d_active.astype(jnp.bfloat16)
    grad_w_inner = jnp.einsum("td,tf->df", normed_low, d_inner, preferred_element_type=jnp.float32)
    grad_inner_bias = jnp.sum(d_inner.astype(jnp.float32), axis=0)
    d_normed = d_second + jnp.einsum(
        "tf,df->td", d_inner, w_inner, preferred_element_type=jnp.float32
    )
    inner_total = lax.psum(grad_inner_bias, ("seq", "rows"))
    d_first, d_gain_one, d_shift_one = first_back(d_normed)
    d_attended = d_first.astype(jnp.bfloat16)
    grad_w_output = jnp.einsum(
        "tc,td->cd", context_low, d_attended, preferred_element_type=jnp.float32
    )
    d_context = jnp.einsum(
        "td,cd->tc", d_attended, w_output, preferred_element_type=jnp.float32
    ).astype(jnp.bfloat16)
    back_items = items + (by_head(d_context, block), log_total)
    d_query_heads, d_keys_heads, d_values_heads, d_reversed, d_pos_shifted = lax.map(
        partial(attend_back, valid=valid, scale=scale), back_items
    )
    d_query = from_heads(d_query_heads, block).astype(jnp.bfloat16)
    d_keys_window = from_heads(d_keys_heads, window).reshape(count, window, width)
    d_values_window = from_heads(d_values_heads, window).reshape(count, window, width)
    d_pairs = jnp.concatenate([d_keys_window, d_values_window], axis=2)
    from_next = shifted(d_pairs[:, :span].astype(jnp.bfloat16), "seq", -1).astype(jnp.float32)
    from_prev = shifted(d_pairs[:, span + block :], "seq", 1)
    middle = d_pairs[:, span : span + block]
    middle = middle + jnp.pad(from_prev, ((0, 0), (0, block - span), (0, 0)))
    middle = middle + jnp.pad(from_next, ((0, 0), (block - span, 0), (0, 0)))
    d_pairs_low = middle.reshape(tokens, 2 * width).astype(jnp.bfloat16)
    d_keys = d_pairs_low[:, :width]
    d_values = d_pairs_low[:, width:]
    grad_w_query = jnp.einsum("tc,td->cd", flat_in, d_query, preferred_element_type=jnp.float32)
    grad_w_key = jnp.einsum("tc,td->cd", flat_in, d_keys, preferred_element_type=jnp.float32)
    grad_w_value = jnp.einsum("tc,td->cd", flat_in, d_values, preferred_element_type=jnp.float32)
    d_hidden = d_first + jnp.einsum(
        "td,cd->tc", d_query, w_query, preferred_element_type=jnp.float32
    )
    d_hidden = d_hidden + jnp.einsum("td,cd->tc", d_keys, w_key, preferred_element_type=jnp.float32)
    d_hidden = d_hidden + jnp.einsum(
        "td,cd->tc", d_values, w_value, preferred_element_type=jnp.float32
    )
    grad_hidden = d_hidden.astype(jnp.bfloat16).reshape(count, block, width)
    d_pos_keys = table_sum(d_reversed)[::-1]
    shift_rows = table_sum(d_pos_shifted)
    d_pos_queries = jnp.concatenate(
        [
            jnp.zeros((1, width), jnp.float32),
            shift_rows[: 2 * span - 2],
            shift_rows[2 * span - 2 : 2 * span - 1] + shift_rows[2 * span - 1 :],
        ],
        axis=0,
    )
    rel_full = rel_table.astype(jnp.float32)
    full_pos_key = jnp.dot(rel_full.T, d_pos_keys, precision=highest)
    full_pos_query = jnp.dot(rel_full.T, d_pos_queries, precision=highest)
    full_rel = jnp.dot(d_pos_keys, w_pos_key.astype(jnp.float32).T, precision=highest)
    full_rel = full_rel + jnp.dot(
        d_pos_queries, w_pos_query.astype(jnp.float32).T, precision=highest
    )
    grad_rel, grad_w_pos_key, grad_w_pos_query = (
        lax.psum_scatter(
            full_rel.astype(jnp.bfloat16), "rows", scatter_dimension=1, tiled=True
        ).astype(jnp.float32),
        lax.psum_scatter(
            full_pos_key.astype(jnp.bfloat16), "rows", scatter_dimension=0, tiled=True
        ).astype(jnp.float32),
        lax.psum_scatter(
            full_pos_query.astype(jnp.bfloat16), "rows", scatter_dimension=0, tiled=True
        ).astype(jnp.float32),
    )
    grad_biases = jnp.stack(
        [
            jnp.sum(d_query.astype(jnp.float32), axis=0),
            jnp.sum(d_values.astype(jnp.float32), axis=0),
            jnp.sum(d_pos_queries, axis=0),
            jnp.sum(d_attended.astype(jnp.float32), axis=0),
        ]
    )
    grad_gains = jnp.stack([d_gain_one, d_gain_two])
    grad_shifts = jnp.stack([d_shift_one, d_shift_two])
    summed = (
        lax.psum_scatter(
            grad_w_query.astype(jnp.bfloat16), "rows", scatter_dimension=0, tiled=True
        ).astype(jnp.float32),
        lax.psum_scatter(
            grad_w_key.astype(jnp.bfloat16), "rows", scatter_dimension=0, tiled=True
        ).astype(jnp.float32),
        lax.psum_scatter(
            grad_w_value.astype(jnp.bfloat16), "rows", scatter_dimension=0, tiled=True
        ).astype(jnp.float32),
        lax.psum_scatter(
            grad_w_output.astype(jnp.bfloat16), "rows", scatter_dimension=0, tiled=True
        ).astype(jnp.float32),
        lax.psum_scatter(
            grad_biases.astype(jnp.bfloat16), "rows", scatter_dimension=1, tiled=True
        ).astype(jnp.float32),
        lax.psum_scatter(
            grad_gains.astype(jnp.bfloat16), "rows", scatter_dimension=1, tiled=True
        ).astype(jnp.float32),
        lax.psum_scatter(
            grad_shifts.astype(jnp.bfloat16), "rows", scatter_dimension=1, tiled=True
        ).astype(jnp.float32),
        lax.psum_scatter(
            grad_w_inner.astype(jnp.bfloat16), "rows", scatter_dimension=0, tiled=True
        ).astype(jnp.float32),
        lax.psum_scatter(
            grad_w_outer.astype(jnp.bfloat16), "rows", scatter_dimension=1, tiled=True
        ).astype(jnp.float32),
        lax.psum_scatter(
            grad_outer_bias.astype(jnp.bfloat16), "rows", scatter_dimension=0, tiled=True
        ).astype(jnp.float32),
    )
    rest_part = tuple(summed[:7])
    ffn_part = tuple(summed[7:])
    totals = (
        lax.psum(rest_part[0].astype(jnp.bfloat16), "seq").astype(jnp.float32),
        lax.psum(rest_part[1].astype(jnp.bfloat16), "seq").astype(jnp.float32),
        lax.psum(rest_part[2].astype(jnp.bfloat16), "seq").astype(jnp.float32),
        lax.psum(rest_part[3].astype(jnp.bfloat16), "seq").astype(jnp.float32),
        lax.psum(grad_rel.astype(jnp.bfloat16), "seq").astype(jnp.float32),
        lax.psum(grad_w_pos_key.astype(jnp.bfloat16), "seq").astype(jnp.float32),
        lax.psum(grad_w_pos_query.astype(jnp.bfloat16), "seq").astype(jnp.float32),
        lax.psum(rest_part[4].astype(jnp.bfloat16), "seq").astype(jnp.float32),
        lax.psum(rest_part[5].astype(jnp.bfloat16), "seq").astype(jnp.float32),
        lax.psum(rest_part[6].astype(jnp.bfloat16), "seq").astype(jnp.float32),
        lax.psum(ffn_part[0].astype(jnp.bfloat16), "seq").astype(jnp.float32),
        lax.psum(ffn_part[1].astype(jnp.bfloat16), "seq").astype(jnp.float32),
        lax.psum(ffn_part[2].astype(jnp.bfloat16), "seq").astype(jnp.float32),
    )
    totals = tuple(totals)
    return (result, grad_hidden) + totals[:10] + (totals[10], inner_total, totals[11], totals[12])


def solution(mesh):
    in_specs = (
        P("rows", "seq", None),
        P("rows", "seq", None),
        P("rows", "seq"),
        P(),
        P(),
        P(),
        P(),
        P(),
        P(),
        P(),
        P(),
        P(),
        P(),
        P(),
        P(),
        P(),
        P(),
    )
    out_specs = (
        P("rows", "seq", None),
        P("rows", "seq", None),
        P("rows", None),
        P("rows", None),
        P("rows", None),
        P("rows", None),
        P(None, "rows"),
        P("rows", None),
        P("rows", None),
        P(None, "rows"),
        P(None, "rows"),
        P(None, "rows"),
        P("rows", None),
        P(),
        P(None, "rows"),
        P("rows"),
    )
    return jax.shard_map(local, mesh=mesh, in_specs=in_specs, out_specs=out_specs, check_vma=False)
```

profile of v0, /device:TPU:0, one launch (start us, length us, event | category | flops | bytes accessed | tf_op | source)
XLA Modules:
  0.0 993.2 jit_solution(13927522806852209937)
XLA Ops:
  12.2 4.9 collective-permute-start
  37.8 145.8 %while.38 = (s32[]{:T(128)}, bf16[6,512,64]{1,2,0:T(8,128)(2,1)}, f32[6,512]{1,0:T(8,128)}, bf16[6,512,64]{2,1,0:T(8,128)(2,1)}, bf16[6,1024,64]{2,1,0:T(8,128)(...) while((s32[]{:T(128)}, bf16[6,512,64]{1,2,0:T(8,128)(2,1)}, ...), condition=%wide.region_3.4_spmd.clone.clone, body=%wide.region_0.3_spmd.clone.sunk.clone | while | flops 238812672 | bytes 51816572 | solution.py:192
  40.4 3.0 reshape.475
  97.0 3.0 reshape.474
  121.2 3.0 reshape.474
  137.3 3.0 reshape.475
  145.5 3.0 reshape.474
  161.6 3.0 reshape.475
  169.7 3.0 reshape.474
  185.6 7.6 multiply_convert_fusion.1
  204.6 355.4 %while.39 = (s32[]{:T(128)}, bf16[6,512,64]{1,2,0:T(8,128)(2,1)}, f32[6,1024,64]{1,2,0:T(8,128)}, f32[6,1024,64]{1,2,0:T(8,128)}, f32[6,512,64]{1,2,0:T(8,128)},...) while((s32[]{:T(128)}, bf16[6,512,64]{1,2,0:T(8,128)(2,1)}, ...), condition=%wide.region_14.15_spmd.clone.clone, body=%wide.region_12.14_spmd.clone.sunk.clone | while | flops 642088448 | bytes 102420696 | solution.py:230
  207.3 3.0 reshape.480
  215.4 3.0 reshape.479
  246.2 3.5 reshape.485
  305.4 3.5 reshape.485
  364.6 3.5 reshape.485
  423.7 3.5 reshape.485
  482.9 3.5 reshape.485
  542.0 3.5 reshape.485
  564.4 6.2 collective-permute-start.2
  573.0 5.6 rev.7
  594.0 3.3 convolution_convert_fusion
  600.1 41.5 %psum.109 = f32[1536]{0:T(1024)} all-reduce(f32[1536]{0:T(1024)S(1)} %copy-done.40), channel_id=1, replica_groups=mesh['seq'=2,'rows'=16] {'seq','rows'}, use_global_device_ids=true, to_apply=%region_46.47 | all-reduce | flops 1536 | bytes 12288 | tf_op jit(solution)/shard_map/psum | solution.py:220
  641.6 3.3 convolution_convert_fusion.1
  646.7 32.2 %all-reduce.25 = (bf16[4,384]{1,0:T(4,128)(2,1)S(1)}, bf16[2,384]{1,0:T(2,128)(2,1)S(1)}, bf16[2,384]{1,0:T(2,128)(2,1)S(1)}, bf16[384]{0:T(512)(128)(2,1)S(1)}) all-reduce(bf16[4,384]{1,0:T(4,128)(2,1)S(1)} %pad_maximum_fusion.6, bf16[2,384]{1,0:T(2,128)(2,1)S(1)} %pad_maximum_fusion.7, ...), channel_id=9, replica_groups=mesh['seq'=2,'rows'=16] {'rows'}, use_global_device_ids=true, to_apply=%region_33.34.clone | all-reduce | flops 3456 | bytes 13824
  681.3 7.3 all-reduce.33.cloned.1.call-done
  696.9 48.3 %reduce-scatter.21.cloned.1.call-done = bf16[24,384]{1,0:T(8,128)(2,1)} async-done(((bf16[384,384]{1,0:T(8,128)(2,1)}), bf16[24,384]{1,0:T(8,128)(2,1)}) %reduce-scatter.21.cloned.1.call-update) | async-done | bytes 18448
  745.3 59.1 %reduce-scatter.15.cloned.1.call-done = bf16[512,24]{0,1:T(8,128)(2,1)} async-done(((bf16[512,384]{0,1:T(8,128)(2,1)}), bf16[512,24]{0,1:T(8,128)(2,1)}) %reduce-scatter.15.cloned.1.call-update) | async-done | bytes 24592 | tf_op jit(solution)/shard_map/reduce_scatter | solution.py:274
  804.8 60.1 %reduce-scatter.19.cloned.1.call-done = bf16[1536,24]{0,1:T(8,128)(2,1)} async-done(((bf16[1536,384]{0,1:T(8,128)(2,1)}), bf16[1536,24]{0,1:T(8,128)(2,1)}) %reduce-scatter.19.cloned.1.call-update) | async-done | bytes 73744 | tf_op jit(solution)/shard_map/reduce_scatter | solution.py:319
  864.9 60.6 %reduce-scatter.17.cloned.1.call-done = bf16[24,1536]{1,0:T(8,128)(2,1)} async-done(((bf16[384,1536]{1,0:T(8,128)(2,1)}), bf16[24,1536]{1,0:T(8,128)(2,1)}) %reduce-scatter.17.cloned.1.call-update) | async-done | bytes 73744 | tf_op jit(solution)/shard_map/reduce_scatter | solution.py:316
  929.7 29.0 %all-reduce.35.cloned.1.call-done = (bf16[24,384]{0,1:T(8,128)(2,1)}, bf16[24,384]{0,1:T(8,128)(2,1)}, bf16[24,384]{0,1:T(8,128)(2,1)}, bf16[24,384]{0,1:T(8,128...) async-done(((bf16[24,384]{0,1:T(8,128)(2,1)}, ...) | async-done | bytes 135616 | tf_op jit(solution)/shard_map/psum | solution.py:329
  974.2 8.8 all-reduce.37.cloned.1.call-done
  (635 shorter events, 549.3 us)
Async XLA Ops:
  7.2 178.3 %copy-start = (bf16[384,1536]{1,0:T(8,128)(2,1)S(1)}, bf16[384,1536]{1,0:T(8,128)(2,1)}, u32[]{:S(2)}) copy-start(bf16[384,1536]{1,0:T(8,128)(2,1)} %param.34) | copy-start | bytes 3538948
  7.2 681.4 %all-reduce.33.cloned.1.call-start = ((), (), s32[]{:S(2)}) async-start(), calls=%async_computation.8 | async-start | bytes 2949120
  9.5 8.8 copy-start.21
  9.6 8.8 copy-start.33
  11.2 7.7 copy-start.27
  11.2 8.1 copy-start.16
  11.2 8.1 copy-start.32
  12.2 21.2 %collective-permute-start = (bf16[1,256,768]{1,2,0:T(8,128)(2,1)}, bf16[1,256,768]{1,2,0:T(8,128)(2,1)S(1)}, u32[]{:S(2)}, u32[]{:S(2)}) collective-permute-start(bf16[1,256,768]{1,2,0:T(8,128)(2,1)} %get-tuple-element.569), channel_id=1, source_target_pairs={{0,16},{1,17},{2,18},{3,19},{4,20},{5,21},{6,22},{7,23},{8,24},{9,... | collective-permute-start | bytes 1179656 | tf_op jit(solution)/shard_map/ppermute | solution.py:22
  17.1 16.3 %collective-permute-start.1 = (bf16[1,256,768]{1,2,0:T(8,128)(2,1)}, bf16[1,256,768]{1,2,0:T(8,128)(2,1)}, u32[]{:S(2)}, u32[]{:S(2)}) collective-permute-start(bf16[1,256,768]{1,2,0:T(8,128)(2,1)} %get-tuple-element.570), channel_id=1, source_target_pairs={{16,0},{17,1},{18,2},{19,3},{20,4},{21,5},{22,6},{23,7},{24,8},{25... | collective-permute-start | bytes 1179656 | tf_op jit(solution)/shard_map/ppermute | solution.py:25
  25.7 6.5 copy-start.53
  185.3 16.6 %copy-start.8 = (f32[512,384]{0,1:T(8,128)}, f32[512,384]{0,1:T(8,128)S(1)}, u32[]{:S(2)}) copy-start(f32[512,384]{0,1:T(8,128)S(1)} %get-tuple-element.574) | copy-start | bytes 2359300
  185.5 16.5 %copy-start.43 = (f32[512]{0:T(512)}, f32[512]{0:T(512)S(1)}, u32[]{:S(2)}) copy-start(f32[512]{0:T(512)S(1)} %fusion.137) | copy-start | bytes 6148
  185.5 7.7 copy-start.52
  185.6 7.7 copy-start.57
  562.2 9.6 copy-start.7
  562.3 9.6 copy-start.17
  564.4 21.8 %collective-permute-start.2 = (f32[1,256,768]{1,2,0:T(8,128)}, f32[1,256,768]{1,2,0:T(8,128)}, u32[]{:S(2)}, u32[]{:S(2)}) collective-permute-start(f32[1,256,768]{1,2,0:T(8,128)} %fusion.112), channel_id=1, source_target_pairs={{0,16},{1,17},{2,18},{3,19},{4,20},{5,21},{6,22},{7,23},{8,24},{9,... | collective-permute-start | bytes 2359304 | tf_op jit(solution)/shard_map/ppermute | solution.py:33
  570.5 14.3 %collective-permute-start.3 = (bf16[1,256,768]{1,2,0:T(8,128)(2,1)}, bf16[1,256,768]{1,2,0:T(8,128)(2,1)}, u32[]{:S(2)}, u32[]{:S(2)}) collective-permute-start(bf16[1,256,768]{1,2,0:T(8,128)(2,1)} %fusion.113), channel_id=1, source_target_pairs={{16,0},{17,1},{18,2},{19,3},{20,4},{21,5},{22,6},{23,7},{24,8},{25... | collective-permute-start | bytes 1179656 | tf_op jit(solution)/shard_map/ppermute | solution.py:33
  571.9 8.8 copy-start.36
  578.6 7.6 copy-start.5
  590.0 155.3 %reduce-scatter.21.cloned.1.call-start = ((), (), s32[]{:S(2)}) async-start(), calls=%async_computation.7 | async-start | bytes 313344
  591.2 213.2 %reduce-scatter.15.cloned.1.call-start = ((), (), s32[]{:S(2)}) async-start(), calls=%async_computation.4 | async-start | bytes 417792 | tf_op jit(solution)/shard_map/reduce_scatter | solution.py:274
  594.0 271.0 %reduce-scatter.19.cloned.1.call-start = ((), (), s32[]{:S(2)}) async-start(), calls=%async_computation.6 | async-start | bytes 1253376 | tf_op jit(solution)/shard_map/reduce_scatter | solution.py:319
  597.3 44.3 %copy-start.9 = (f32[512,384]{0,1:T(8,128)S(1)}, f32[512,384]{0,1:T(8,128)}, u32[]{:S(2)}) copy-start(f32[512,384]{0,1:T(8,128)} %copy-done.8) | copy-start | bytes 2359300
  597.3 44.3 %copy-start.42 = (f32[384]{0:T(512)S(1)}, f32[384]{0:T(512)}, u32[]{:S(2)}) copy-start(f32[384]{0:T(512)} %get-tuple-element.581) | copy-start | bytes 4612
  597.3 44.3 %copy-start.44 = (f32[512]{0:T(512)S(1)}, f32[512]{0:T(512)}, u32[]{:S(2)}) copy-start(f32[512]{0:T(512)} %copy-done.43) | copy-start | bytes 6148
  597.3 44.3 %copy-start.51 = (f32[384]{0:T(512)S(1)}, f32[384]{0:T(512)}, u32[]{:S(2)}) copy-start(f32[384]{0:T(512)} %get-tuple-element.477) | copy-start | bytes 4612
  597.3 328.2 %reduce-scatter.17.cloned.1.call-start = ((), (), s32[]{:S(2)}) async-start(), calls=%async_computation.5 | async-start | bytes 1253376 | tf_op jit(solution)/shard_map/reduce_scatter | solution.py:316
  645.0 313.7 %all-reduce.35.cloned.1.call-start = ((), (), s32[]{:S(2)}) async-start(), calls=%async_computation.9 | async-start | bytes 1074176 | tf_op jit(solution)/shard_map/psum | solution.py:329
  645.1 159.3 %copy-start.35 = (bf16[384,384]{1,0:T(8,128)(2,1)S(1)}, bf16[384,384]{1,0:T(8,128)(2,1)}, u32[]{:S(2)}) copy-start(bf16[384,384]{1,0:T(8,128)(2,1)} %param.26) | copy-start | bytes 884740
  804.4 178.7 %all-reduce.37.cloned.1.call-start = ((), (), s32[]{:S(2)}) async-start(), calls=%async_computation.10 | async-start | bytes 294912 | tf_op jit(solution)/shard_map/psum | solution.py:339
  925.6 60.6 %copy-start.1 = (bf16[384,1536]{1,0:T(8,128)(2,1)S(1)}, bf16[384,1536]{1,0:T(8,128)(2,1)}, u32[]{:S(2)}) copy-start(bf16[384,1536]{1,0:T(8,128)(2,1)} %param.34) | copy-start | bytes 3538948
  (63 other events, 145.6 us)
Sparse Core Ops, SparseCore 0:
  590.1 98.4 all-reduce.32
  692.1 53.1 reduce-scatter.20
  749.8 54.5 reduce-scatter.14
  807.8 57.0 reduce-scatter.18
  868.4 57.1 reduce-scatter.16
  928.9 29.7 all-reduce.34
  961.1 21.8 all-reduce.36
where the time goes:
time: 1000 us; the launch traced here: 993 us
  local copies, waits for them, and re-layouts  379 us (38%)
  waiting for transfers between devices  275 us (28%)
  matrix products  198 us (20%)
  blocking collectives  73.7 us (7%)
  other arithmetic  36 us (4%)
  between operations  16 us (2%)
  starting transfers between devices  13.9 us (1%)
    reshape x30, local copies, waits for them, and re-layouts, to_band(): return flat.reshape(height, length + 1)[:, :columns]  90.5 us
    reduce_scatter x1, waiting for transfers between devices, local(): lax.psum_scatter(grad_w_inner.astype(jnp.bfloat16), 'rows', scatter_dimen...  60.6 us
    reduce_scatter x1, waiting for transfers between devices, local(): lax.psum_scatter(grad_w_outer.astype(jnp.bfloat16), 'rows', scatter_dimen...  60.1 us
    reduce_scatter x1, waiting for transfers between devices, local(): lax.psum_scatter(full_rel.astype(jnp.bfloat16), 'rows', scatter_dimension...  59.1 us
    unnamed x9, waiting for transfers between devices  55.7 us
    reshape x24, local copies, waits for them, and re-layouts, from_band(): flat = jnp.pad(padded.reshape(height * (length + 1)), (1, 0))  50.7 us
    slice x24, local copies, waits for them, and re-layouts, from_band(): return flat[:height * length].reshape(height, length)  49.1 us
    while x78, local copies, waits for them, and re-layouts  41.9 us
  transfers between devices with their start and end apart: 11, of which 8 were waited for; matrix products, arithmetic and copies ran while one was open for 7% of the time, Pallas kernels for 0%

commit v1 on v0

v1 whole, which is shorter than its diff:
```python
from functools import partial
import math

import jax
import jax.numpy as jnp
import numpy as np
from jax import lax
from jax.experimental import pallas as pl
from jax.experimental.pallas import tpu as pltpu
from jax.sharding import PartitionSpec as P

HEADS = 6
PAIRS = HEADS // 2
TILE = 128
norm_eps = 1e-07
masked_score = -1e30
f32 = jnp.float32
bf16 = jnp.bfloat16
MiB = 1 << 20


def nn(left, right):
    return lax.dot_general(left, right, (((1,), (0,)), ((), ())), preferred_element_type=f32)


def nt(left, right):
    return lax.dot_general(left, right, (((1,), (1,)), ((), ())), preferred_element_type=f32)


def iota(shape, axis):
    return lax.broadcasted_iota(jnp.int32, shape, axis)


def where_bf16(mask, value):
    return jnp.where(mask, value.astype(f32), 0.0).astype(bf16)


def skew(block, first):
    return pltpu.roll(block, first, 1, stride=1, stride_axis=0)


def exchange(value, axis, bit):
    count = lax.axis_size(axis)
    return lax.ppermute(value, axis, [(i, i ^ bit) for i in range(count)])


def project_kernel(
    info,
    x,
    x_low,
    x_high,
    w_query,
    w_key,
    w_value,
    rel,
    w_pos_key,
    w_pos_query,
    biases,
    places,
    q_out,
    k_out,
    v_out,
    pk_out,
    pk_rev_out,
    pq_rev_out,
    order_out,
):
    def split(out, first, value):
        rows = value.shape[0]
        for p in range(PAIRS):
            out[p, first : first + rows, :] = value[:, p * TILE : (p + 1) * TILE].astype(bf16)

    bias = biases[...].astype(f32)
    block = x.shape[0]
    span = x_low.shape[0]
    split(q_out, 0, nn(x[...], w_query[...]) + bias[0:1])
    for first, source in ((0, x_low), (span, x), (span + block, x_high)):
        split(k_out, first, nn(source[...], w_key[...]))
        split(v_out, first, nn(source[...], w_value[...]) + bias[1:2])
    count = rel.shape[0]
    pos_keys = nn(rel[...], w_pos_key[...]).astype(bf16)
    pos_queries = (nn(rel[...], w_pos_query[...]) + bias[2:3]).astype(bf16)
    row, col = iota((count, count), 0), iota((count, count), 1)
    flip = jnp.where(col == count - 1 - row, 1.0, 0.0).astype(bf16)
    pick = jnp.where(col == jnp.minimum(count - row, count - 1), 1.0, 0.0).astype(bf16)
    split(pk_out, 0, pos_keys)
    split(pk_rev_out, 0, nn(flip, pos_keys))
    split(pq_rev_out, 0, nn(pick, pos_queries))
    width = order_out.shape[0]
    shard = jnp.bitwise_xor(places[:, 0:1], info[2])
    target = shard * places[0, 2] + places[:, 1:2]
    order_out[...] = jnp.where(iota((width, width), 1) == target, 1.0, 0.0).astype(bf16)


def key_block_range(wb, blocks, tiles):
    low, high = max(0, blocks - 1 - wb), min(blocks - 1, tiles + blocks - 2 - wb)
    return low, high, max(low - 1, 0), min(high, blocks - 2)


def attend_kernel(info, q, k, v, pk_rev, pq_rev, context, probs, from_scr, *, scale):
    row, lane = iota((TILE, TILE), 0), iota((TILE, TILE), 1)
    eye = jnp.where(row == lane, 1.0, 0.0).astype(bf16)
    halves = (lane < TILE // 2, lane >= TILE // 2)
    tiles = q.shape[1] // TILE
    blocks = pk_rev.shape[1] // TILE + 1
    side = blocks // 2
    tables = []
    for h in range(2):
        table = pq_rev[0].astype(f32)
        half = iota((table.shape[0], TILE), 1) // (TILE // 2) == h
        tables.append(jnp.where(half, table, 0.0).astype(bf16))
    for wb in range(tiles + blocks - 1):
        low, high, first, last = key_block_range(wb, blocks, tiles)
        kb = k[0, wb * TILE : (wb + 1) * TILE, :]
        for h in range(2):
            product = nt(kb, tables[h][first * TILE : (last + 1) * TILE])
            turned = {}
            for a in range(first, last + 1):
                turned[a] = skew(product[:, (a - first) * TILE : (a - first + 1) * TILE], 0)
            for e in range(low, high + 1):
                if e == 0:
                    term = turned[0]
                elif e == blocks - 1:
                    term = turned[blocks - 2]
                else:
                    term = jnp.where(lane >= row, turned[e], turned[e - 1])
                it, b = wb - (blocks - 1) + e, blocks - 1 - e
                from_scr[h, it, b] = term.astype(bf16)
    before = jnp.where(info[0] == 0, masked_score, 0.0)
    after = jnp.where(info[0] == info[1] - 1, masked_score, 0.0)
    rate = scale * math.log2(math.e)
    for it in range(tiles):
        qt = q[0, it * TILE : (it + 1) * TILE, :]
        parts = []
        for h in range(2):
            qh = where_bf16(halves[h], qt)
            product = nt(qh, pk_rev[0])
            turned = [
                skew(product[:, b * TILE : (b + 1) * TILE], 1) for b in range(blocks - 1)
            ]
            left = jnp.concatenate([qh, eye], axis=1)
            scores = []
            for b in range(blocks):
                wb = it + b
                right = jnp.concatenate(
                    [k[0, wb * TILE : (wb + 1) * TILE, :], from_scr[h, it, b]], axis=1
                )
                score = nt(left, right)
                if b == 0:
                    score = jnp.where(lane > row, score + turned[0], masked_score)
                elif b == blocks - 1:
                    score = jnp.where(lane <= row, score + turned[b - 1], masked_score)
                else:
                    score = score + jnp.where(lane > row, turned[b], turned[b - 1])
                if wb < side:
                    score = score + before
                if wb >= side + tiles:
                    score = score + after
                scores.append(score)
            largest = scores[0]
            for score in scores[1:]:
                largest = jnp.maximum(largest, score)
            largest = jnp.max(largest, axis=1, keepdims=True)
            weights = [jnp.exp2((score - largest) * rate) for score in scores]
            total = weights[0]
            for weight in weights[1:]:
                total = total + weight
            inverse = 1.0 / jnp.sum(total, axis=1, keepdims=True)
            low_probs = jnp.concatenate([(w * inverse).astype(bf16) for w in weights], axis=1)
            probs[0, h, it] = low_probs
            parts.append(nn(low_probs, v[0, it * TILE : (it + blocks) * TILE, :]))
        context[it * TILE : (it + 1) * TILE, :] = jnp.where(halves[0], parts[0], parts[1]).astype(
            bf16
        )


def attend_back_kernel(
    q,
    k,
    v,
    pk,
    pq_rev,
    d_context,
    context,
    probs,
    dq_out,
    dk_out,
    dv_out,
    dpk_out,
    dpq_out,
    turn_scr,
    dk_scr,
    dv_scr,
    dpk_scr,
    dpq_scr,
    *,
    scale,
):
    row, lane = iota((TILE, TILE), 0), iota((TILE, TILE), 1)
    flip = jnp.where(row + lane == TILE - 1, 1.0, 0.0).astype(bf16)
    row2, lane2 = iota((2 * TILE, 2 * TILE), 0), iota((2 * TILE, 2 * TILE), 1)
    same = (row2 // TILE) == (lane2 // TILE)
    flip2 = jnp.where(
        same & (row2 % TILE + lane2 % TILE == TILE - 1), 1.0, 0.0
    ).astype(bf16)
    halves = (lane < TILE // 2, lane >= TILE // 2)
    row_halves = (row < TILE // 2, row >= TILE // 2)
    tiles = q.shape[1] // TILE
    blocks = pk.shape[1] // TILE + 1
    tables = []
    for h in range(2):
        table = pq_rev[0].astype(f32)
        half = iota((table.shape[0], TILE), 1) // (TILE // 2) == h
        tables.append(jnp.where(half, table, 0.0).astype(bf16))

    def turned_pair(value):
        flat = value.astype(f32).T
        return jnp.concatenate(
            [jnp.where(row_halves[h], flat, 0.0).astype(bf16) for h in range(2)], axis=1
        )

    dk_scr[...] = jnp.zeros_like(dk_scr)
    dv_scr[...] = jnp.zeros_like(dv_scr)
    dpk_scr[...] = jnp.zeros_like(dpk_scr)
    dpq_scr[...] = jnp.zeros_like(dpq_scr)
    for it in range(tiles):
        rows = slice(it * TILE, (it + 1) * TILE)
        window = slice(it * TILE, (it + blocks) * TILE)
        qt, dct = q[0, rows, :], d_context[rows, :]
        overlap = dct.astype(f32) * context[rows, :].astype(f32)
        d_raw, bands, parts, heads_q = [], [], [], []
        for h in range(2):
            d_probs = nt(where_bf16(halves[h], dct), v[0, window, :])
            delta = jnp.sum(jnp.where(halves[h], overlap, 0.0), axis=1, keepdims=True)
            p = probs[0, h, it].astype(f32)
            ds = p * (d_probs - delta) * scale
            ds_low = ds.astype(bf16)
            part = nn(ds_low, k[0, window, :])
            merged = [
                jnp.where(
                    lane > row,
                    ds[:, b * TILE : (b + 1) * TILE],
                    ds[:, (b + 1) * TILE : (b + 2) * TILE],
                ).astype(bf16)
                for b in range(blocks - 1)
            ]
            band = [None] * (blocks - 1)
            for b in range(0, blocks - 1, 2):
                flipped = nn(jnp.concatenate(merged[b : b + 2], axis=1), flip2)
                for c in range(2):
                    band[blocks - 2 - b - c] = skew(
                        flipped[:, c * TILE : (c + 1) * TILE], 1
                    ).astype(bf16)
            band = jnp.concatenate(band, axis=1)
            part = part + nn(band, pk[0])
            d_raw.append(ds_low)
            bands.append(band)
            parts.append(part)
            heads_q.append(where_bf16(halves[h], qt))
        dq_out[rows, :] = jnp.where(halves[0], parts[0], parts[1]).astype(bf16)
        q_turned, dc_turned = turned_pair(qt), turned_pair(dct)
        dpk_scr[...] += nn(q_turned, jnp.concatenate(bands, axis=0))
        dv_scr[:, window] += nn(
            dc_turned, jnp.concatenate([probs[0, 0, it], probs[0, 1, it]], axis=0)
        )
        stacked_q = jnp.concatenate(heads_q, axis=0)
        both = jnp.concatenate(d_raw, axis=0)
        for b in range(blocks):
            wb = it + b
            turned = nt(flip, both[:, b * TILE : (b + 1) * TILE]).astype(bf16)
            turn_scr[it, b] = turned
            dk_scr[wb * TILE : (wb + 1) * TILE, :] += nn(turned, stacked_q)
    for wb in range(tiles + blocks - 1):
        low, high, first, last = key_block_range(wb, blocks, tiles)
        rows = slice(wb * TILE, (wb + 1) * TILE)

        def source(e, h):
            if e < low or e > high:
                return jnp.zeros((TILE, TILE), f32)
            it, b = wb - (blocks - 1) + e, blocks - 1 - e
            return turn_scr[it, b, :, h * TILE : (h + 1) * TILE].astype(f32)

        bands, total = [], None
        for h in range(2):
            pieces = []
            for a in range(first, last + 1):
                merged = jnp.where(lane + row >= TILE - 1, source(a, h), source(a + 1, h))
                pieces.append(skew(merged, 1).astype(bf16))
            band = jnp.concatenate(pieces, axis=1)
            bands.append(band)
            part = nn(band, tables[h][first * TILE : (last + 1) * TILE])
            total = part if total is None else total + part
        dk_low = (dk_scr[rows, :] + total).astype(bf16)
        dk_out[rows, :] = nn(flip, dk_low).astype(bf16)
        k_turned = nn(k[0, rows, :].astype(f32).T.astype(bf16), flip)
        k_turned = jnp.concatenate(
            [jnp.where(row_halves[h], k_turned, 0.0).astype(bf16) for h in range(2)], axis=1
        )
        dpq_scr[:, first * TILE : (last + 1) * TILE] += nn(
            k_turned, jnp.concatenate(bands, axis=0)
        )
        dv_out[rows, :] = dv_scr[:, rows].T.astype(bf16)
    dpk_out[...] = dpk_scr[...].astype(bf16)
    dpq_out[...] = dpq_scr[...].astype(bf16)


def norm_parts(value):
    centre = value - jnp.mean(value, axis=1, keepdims=True)
    rate = lax.rsqrt(jnp.mean(centre * centre, axis=1, keepdims=True) + norm_eps)
    return centre * rate, rate


def norm_back(cotangent, normal, rate):
    return rate * (
        cotangent
        - jnp.mean(cotangent, axis=1, keepdims=True)
        - normal * jnp.mean(cotangent * normal, axis=1, keepdims=True)
    )


def middle_kernel(
    x,
    context,
    grad_out,
    mask,
    w_output,
    biases,
    gains,
    shifts,
    w_inner,
    inner_bias,
    w_outer,
    outer_bias,
    order,
    result,
    d_first_out,
    d_context,
    keep,
    send,
    inner_out,
    rows_out,
    low_scr,
    active_scr,
    d_inner_scr,
    d_outer_scr,
    d_att_scr,
    *,
    step,
):
    tokens, width = x.shape
    units = w_inner.shape[1]
    bias = biases[3:4, :].astype(f32)
    gain_one, gain_two = gains[0:1, :].astype(f32), gains[1:2, :].astype(f32)
    shift_one, shift_two = shifts[0:1, :].astype(f32), shifts[1:2, :].astype(f32)
    in_bias, out_bias = inner_bias[...].astype(f32), outer_bias[...].astype(f32)
    diagonal = iota((TILE, TILE), 0) == iota((TILE, TILE), 1)
    sums = [jnp.zeros((1, width), f32) for _ in range(6)]

    def add(index, value):
        sums[index] = sums[index] + jnp.sum(value, axis=0, keepdims=True)

    for first in range(0, tokens, step):
        rows = slice(first, first + step)
        attended = nn(context[rows, :], w_output[...]) + bias
        n_one, r_one = norm_parts(x[rows, :].astype(f32) + attended)
        normed = n_one * gain_one + shift_one
        low = normed.astype(bf16)
        low_scr[rows, :] = low
        inner = nn(low, w_inner[...]) + in_bias
        cumulative = 0.5 + 0.5 * lax.erf(inner * math.sqrt(0.5))
        active = (inner * cumulative).astype(bf16)
        active_scr[rows, :] = active
        slope = cumulative + inner * jnp.exp(-0.5 * inner * inner) * (1.0 / math.sqrt(2 * math.pi))
        outer = nn(active, w_outer[...]) + out_bias
        n_two, r_two = norm_parts(normed + outer)
        result[rows, :] = (n_two * gain_two + shift_two).astype(bf16)
        columns = []
        for part in range(first, first + step, TILE):
            line = mask[0:1, part : part + TILE].astype(f32)
            columns.append(jnp.sum(jnp.where(diagonal, line, 0.0), axis=1, keepdims=True))
        cotangent = grad_out[rows, :].astype(f32) * jnp.concatenate(columns, axis=0)
        add(0, cotangent * n_two)
        add(1, cotangent)
        d_second = norm_back(cotangent * gain_two, n_two, r_two)
        d_outer = d_second.astype(bf16)
        d_outer_scr[rows, :] = d_outer
        add(2, d_outer.astype(f32))
        d_inner = (nt(d_outer, w_outer[...]) * slope).astype(bf16)
        d_inner_scr[rows, :] = d_inner
        d_normed = d_second + nt(d_inner, w_inner[...])
        add(3, d_normed * n_one)
        add(4, d_normed)
        d_first = norm_back(d_normed * gain_one, n_one, r_one)
        d_first_out[rows, :] = d_first
        d_att = d_first.astype(bf16)
        d_att_scr[rows, :] = d_att
        add(5, d_att.astype(f32))
        d_context[rows, :] = nt(d_att, w_output[...]).astype(bf16)

    half = width // 2

    def put(first, left, right):
        turned = nt(order[...], left).astype(bf16)
        for c in range(0, right.shape[1], width):
            value = nn(turned, right[:, c : c + width]).astype(bf16)
            keep[:, first + c : first + c + width] = value[:half]
            send[:, first + c : first + c + width] = value[half:]

    put(0, low_scr[...], d_inner_scr)
    put(units, d_outer_scr[...], active_scr)
    put(2 * units, context[...], d_att_scr)
    inner_out[...] = nn(jnp.ones((8, tokens), bf16), d_inner_scr[...])
    zero = jnp.zeros((1, width), f32)
    table = [zero, zero, zero, sums[5], sums[3], sums[0], sums[4], sums[1], sums[2]]
    rows_out[...] = jnp.concatenate(table + [zero] * (16 - len(table)), axis=0)


def weight_grad_kernel(
    x, x_low, x_high, rel, w_pos_key, w_pos_query, order, dq, dk, dv, dpk, dpq, rows, keep, send
):
    width = x.shape[1]
    half = width // 2
    span = x_low.shape[0]
    block = x.shape[0]
    count = rel.shape[0]

    def put(first, value):
        value = value.astype(bf16)
        keep[:, first : first + value.shape[1]] = value[:half]
        send[:, first : first + value.shape[1]] = value[half:]

    ord_ = order[...]
    x_low_t = nt(ord_, x_low[...]).astype(bf16)
    x_t = nt(ord_, x[...]).astype(bf16)
    x_high_t = nt(ord_, x_high[...]).astype(bf16)
    put(0, nn(x_t, dq[...]))
    x_all = jnp.concatenate([x_low_t, x_t, x_high_t], axis=1)
    put(width, nn(x_all, dk[...]))
    put(2 * width, nn(x_all, dv[...]))
    rel_t = nt(ord_, rel[...]).astype(bf16)
    put(3 * width, nt(rel_t, dpk[...]))
    row, col = iota((count, count), 0), iota((count, count), 1)
    pick = jnp.where(col == jnp.minimum(count - row, count - 1), 1.0, 0.0).astype(bf16)
    dpq_nat = nn(dpq[...], pick).astype(bf16)
    put(4 * width, nt(rel_t, dpq_nat))
    rel_grad = nn(nn(ord_, w_pos_key[...]).astype(bf16), dpk[...])
    rel_grad = rel_grad + nn(nn(ord_, w_pos_query[...]).astype(bf16), dpq_nat)
    put(5 * width, rel_grad)
    known = rows[...]
    sum_q = nn(jnp.ones((8, block), bf16), dq[...])[0:1]
    sum_v = nn(jnp.ones((8, dv.shape[0]), bf16), dv[...])[0:1]
    sum_p = nt(jnp.ones((8, count), bf16), dpq_nat)[0:1]
    place = iota(known.shape, 0)
    known = jnp.where(place == 0, sum_q, known)
    known = jnp.where(place == 1, sum_v, known)
    known = jnp.where(place == 2, sum_p, known)
    padded = jnp.concatenate([known, jnp.zeros((TILE - known.shape[0], width), f32)], axis=0)
    put(5 * width + count, nt(ord_, padded.astype(bf16)))


def input_grad_kernel(dq, dk, dv, d_first, w_query, w_key, w_value, own, low, high):
    span = low.shape[0]
    block = own.shape[0]

    def halo(rows):
        return nt(dk[rows, :], w_key[...]) + nt(dv[rows, :], w_value[...])

    low[...] = halo(slice(0, span)).astype(bf16)
    high[...] = halo(slice(span + block, 2 * span + block)).astype(bf16)
    own[...] = halo(slice(span, span + block)) + d_first[...] + nt(dq[...], w_query[...])


def final_kernel(mid, mid_other, rest, rest_other, *outs, width, units, count):
    def whole(own, other, first, size):
        cols = slice(first, first + size)
        return own[:, cols].astype(f32) + other[:, cols].astype(f32)

    (g_q, g_k, g_v, g_o, g_rel, g_pk, g_pq, g_bias, g_gain, g_shift, g_in, g_out, g_ob) = outs
    g_in[...] = whole(mid, mid_other, 0, units)
    g_out[...] = whole(mid, mid_other, units, units).T
    g_o[...] = whole(mid, mid_other, 2 * units, width)
    for i, out in enumerate((g_q, g_k, g_v, g_pk, g_pq)):
        out[...] = whole(rest, rest_other, i * width, width)
    g_rel[...] = whole(rest, rest_other, 5 * width, count).T
    lines = whole(rest, rest_other, 5 * width + count, TILE).T
    g_bias[...] = lines[0:4]
    g_gain[...] = lines[4:6]
    g_shift[...] = lines[6:8]
    g_ob[...] = lines[8:9]


def bit_reversed(value, bits):
    out = 0
    for _ in range(bits):
        out = out * 2 + value % 2
        value //= 2
    return out


def whole_spec(array):
    rank = len(array.shape)
    return pl.BlockSpec(array.shape, lambda *_: (0,) * rank)


smem = pl.BlockSpec(memory_space=pltpu.SMEM)


def local(
    hidden,
    grad_out,
    grad_mask,
    w_query,
    w_key,
    w_value,
    w_output,
    rel_table,
    w_pos_key,
    w_pos_query,
    attn_biases,
    norm_gains,
    norm_shifts,
    w_inner,
    inner_bias,
    w_outer,
    outer_bias,
):
    count, block, width = hidden.shape
    tokens = count * block
    table = rel_table.shape[0]
    span = table // 2
    window = block + 2 * span
    units = w_inner.shape[1]
    head = width // HEADS
    scale = 1.0 / math.sqrt(3.0 * head)
    n_rows, n_seq = lax.axis_size("rows"), lax.axis_size("seq")
    row_bits, seq_bits = n_rows.bit_length() - 1, n_seq.bit_length() - 1
    share = width // n_rows
    tiles, blocks = block // TILE, table // TILE + 1
    me_seq, me_rows = lax.axis_index("seq"), lax.axis_index("rows")
    info = jnp.stack([me_seq, jnp.int32(n_seq), me_rows]).astype(jnp.int32)
    x = hidden.reshape(tokens, width)
    shape = jax.ShapeDtypeStruct

    forward = [(i, i + 1) for i in range(n_seq - 1)]
    backward = [(i + 1, i) for i in range(n_seq - 1)]
    x_low = lax.ppermute(x[block - span :], "seq", forward)
    x_high = lax.ppermute(x[:span], "seq", backward)

    places = np.zeros((width, 4), np.int32)
    for i in range(width):
        places[i] = (bit_reversed(i // share, row_bits), i % share, share, 0)

    q3, k3, v3, pk3, pk_rev3, pq_rev3, order = pl.pallas_call(
        project_kernel,
        out_shape=(
            shape((PAIRS, block, TILE), bf16),
            shape((PAIRS, window, TILE), bf16),
            shape((PAIRS, window, TILE), bf16),
            shape((PAIRS, table, TILE), bf16),
            shape((PAIRS, table, TILE), bf16),
            shape((PAIRS, table, TILE), bf16),
            shape((width, width), bf16),
        ),
        in_specs=[smem] + [pl.BlockSpec()] * 11,
        compiler_params=pltpu.CompilerParams(vmem_limit_bytes=40 * MiB),
        name="project",
    )(
        info,
        x,
        x_low,
        x_high,
        w_query,
        w_key,
        w_value,
        rel_table,
        w_pos_key,
        w_pos_query,
        attn_biases,
        jnp.asarray(places),
    )

    def pair(rows):
        return pl.BlockSpec((1, rows, TILE), lambda p: (p, 0, 0))

    def flat(rows):
        return pl.BlockSpec((rows, TILE), lambda p: (0, p))

    def turned(cols):
        return pl.BlockSpec((TILE, cols), lambda p: (p, 0))

    probs_spec = pl.BlockSpec(
        (1, 2, tiles, TILE, blocks * TILE), lambda p: (p, 0, 0, 0, 0)
    )
    context, probs = pl.pallas_call(
        partial(attend_kernel, scale=scale),
        grid=(PAIRS,),
        out_shape=(
            shape((tokens, width), bf16),
            shape((PAIRS, 2, tiles, TILE, blocks * TILE), bf16),
        ),
        in_specs=[smem, pair(block), pair(window), pair(window), pair(table), pair(table)],
        out_specs=(flat(block), probs_spec),
        scratch_shapes=[pltpu.VMEM((2, tiles, blocks, TILE, TILE), bf16)],
        compiler_params=pltpu.CompilerParams(vmem_limit_bytes=40 * MiB),
        name="attend",
    )(info, q3, k3, v3, pk_rev3, pq_rev3)

    mid_cols = 2 * units + width
    result, d_first, d_context, mid_keep, mid_send, inner_sum, rows = pl.pallas_call(
        partial(middle_kernel, step=256),
        out_shape=(
            shape((tokens, width), bf16),
            shape((tokens, width), f32),
            shape((tokens, width), bf16),
            shape((width // 2, mid_cols), bf16),
            shape((width // 2, mid_cols), bf16),
            shape((8, units), f32),
            shape((16, width), f32),
        ),
        scratch_shapes=[
            pltpu.VMEM((tokens, width), bf16),
            pltpu.VMEM((tokens, units), bf16),
            pltpu.VMEM((tokens, units), bf16),
            pltpu.VMEM((tokens, width), bf16),
            pltpu.VMEM((tokens, width), bf16),
        ],
        compiler_params=pltpu.CompilerParams(vmem_limit_bytes=56 * MiB),
        name="middle",
    )(
        x,
        context,
        grad_out.reshape(tokens, width),
        grad_mask,
        w_output,
        attn_biases,
        norm_gains,
        norm_shifts,
        w_inner,
        inner_bias.reshape(1, units),
        w_outer,
        outer_bias.reshape(1, width),
        order,
    )

    dq, dk, dv, dpk, dpq = pl.pallas_call(
        partial(attend_back_kernel, scale=scale),
        grid=(PAIRS,),
        out_shape=(
            shape((block, width), bf16),
            shape((window, width), bf16),
            shape((window, width), bf16),
            shape((width, table), bf16),
            shape((width, table), bf16),
        ),
        in_specs=[
            pair(block),
            pair(window),
            pair(window),
            pair(table),
            pair(table),
            flat(block),
            flat(block),
            probs_spec,
        ],
        out_specs=(flat(block), flat(window), flat(window), turned(table), turned(table)),
        scratch_shapes=[
            pltpu.VMEM((tiles, blocks, TILE, 2 * TILE), bf16),
            pltpu.VMEM((window, TILE), f32),
            pltpu.VMEM((TILE, window), f32),
            pltpu.VMEM((TILE, table), f32),
            pltpu.VMEM((TILE, table), f32),
        ],
        compiler_params=pltpu.CompilerParams(vmem_limit_bytes=40 * MiB),
        name="attend_back",
    )(q3, k3, v3, pk3, pq_rev3, d_context, context, probs)

    rest_cols = 5 * width + table + TILE
    rest_keep, rest_send = pl.pallas_call(
        weight_grad_kernel,
        out_shape=(
            shape((width // 2, rest_cols), bf16),
            shape((width // 2, rest_cols), bf16),
        ),
        compiler_params=pltpu.CompilerParams(vmem_limit_bytes=40 * MiB),
        name="weight_grad",
    )(x, x_low, x_high, rel_table, w_pos_key, w_pos_query, order, dq, dk, dv, dpk, dpq, rows)

    own, to_prev, to_next = pl.pallas_call(
        input_grad_kernel,
        out_shape=(
            shape((tokens, width), f32),
            shape((span, width), bf16),
            shape((span, width), bf16),
        ),
        compiler_params=pltpu.CompilerParams(vmem_limit_bytes=40 * MiB),
        name="input_grad",
    )(dq, dk, dv, d_first, w_query, w_key, w_value)
    from_next = lax.ppermute(to_prev, "seq", backward)
    from_prev = lax.ppermute(to_next, "seq", forward)
    grad_hidden = jnp.concatenate(
        [
            own[:span] + from_prev.astype(f32),
            own[span : block - span],
            own[block - span :] + from_next.astype(f32),
        ],
        axis=0,
    ) if block > 2 * span else jnp.concatenate(
        [own[:span] + from_prev.astype(f32), own[span:] + from_next.astype(f32)], axis=0
    )

    def scattered(keep, send):
        for step in range(row_bits):
            total = keep + exchange(send, "rows", 1 << step)
            half = total.shape[0] // 2
            if step < row_bits - 1:
                keep, send = total[:half], total[half:]
        for step in range(seq_bits - 1):
            total = total + exchange(total, "seq", 1 << step)
        return total, exchange(total, "seq", 1 << (seq_bits - 1))

    inner_total = inner_sum[0:1]
    for step in range(row_bits):
        inner_total = inner_total + exchange(inner_total, "rows", 1 << step)
    for step in range(seq_bits):
        inner_total = inner_total + exchange(inner_total, "seq", 1 << step)

    mid, mid_other = scattered(mid_keep, mid_send)
    rest, rest_other = scattered(rest_keep, rest_send)
    square = shape((share, width), f32)
    grads = pl.pallas_call(
        partial(final_kernel, width=width, units=units, count=table),
        out_shape=(
            square,
            square,
            square,
            square,
            shape((table, share), f32),
            square,
            square,
            shape((4, share), f32),
            shape((2, share), f32),
            shape((2, share), f32),
            shape((share, units), f32),
            shape((units, share), f32),
            shape((1, share), f32),
        ),
        name="final",
    )(mid, mid_other, rest, rest_other)
    return (
        result.reshape(count, block, width),
        grad_hidden.astype(bf16).reshape(count, block, width),
        *grads[:11],
        inner_total.reshape(units),
        grads[11],
        grads[12].reshape(share),
    )


def solution(mesh):
    in_specs = (
        P("rows", "seq", None),
        P("rows", "seq", None),
        P("rows", "seq"),
    ) + (P(),) * 14
    out_specs = (
        P("rows", "seq", None),
        P("rows", "seq", None),
        P("rows", None),
        P("rows", None),
        P("rows", None),
        P("rows", None),
        P(None, "rows"),
        P("rows", None),
        P("rows", None),
        P(None, "rows"),
        P(None, "rows"),
        P(None, "rows"),
        P("rows", None),
        P(),
        P(None, "rows"),
        P("rows"),
    )
    return jax.shard_map(local, mesh=mesh, in_specs=in_specs, out_specs=out_specs, check_vma=False)
```

time: 1000 us -> 158 us (0.16)
  local copies, waits for them, and re-layouts: 379 us -> 19.1 us
  waiting for transfers between devices: 275 us -> 40 us
  matrix products: 198 us -> 0 us
  blocking collectives: 73.7 us -> 0 us
  Pallas kernels: 0 us -> 59.9 us
  other arithmetic: 36 us -> 3.16 us
  starting transfers between devices: 13.9 us -> 33.8 us
  between operations: 16 us -> 1.04 us
    dot_general x114 -> x0, matrix products: 198 us -> none  [the longest x12 25.5 us: raw_scores(): jnp.einsum('id,td->it', query, keys_reversed, preferred_element_type=jnp....]
    reshape x84 -> x2, local copies, waits for them, and re-layouts: 186 us -> 2.53 us  [the longest x1 1.29 us: local(): inner_bias.reshape(1, units)]
    reduce_scatter x3 -> x0, waiting for transfers between devices: 180 us -> none  [the longest x1 60.6 us: local(): lax.psum_scatter(grad_w_inner.astype(jnp.bfloat16), 'rows', scatter_dimen...]
    slice x96 -> x8, local copies, waits for them, and re-layouts: 91.2 us -> 2.01 us  [the longest x1 1.06 us: local(): x_high = lax.ppermute(x[:span], 'seq', backward)]
    pallas_call x0 -> x7, Pallas kernels: none -> 59.9 us  [the longest x1 22.6 us: local(): pl.pallas_call(partial(attend_back_kernel, scale=scale), grid=(PAIRS,), o...]
    unnamed x9 -> x0, waiting for transfers between devices: 55.7 us -> none
    while x78 -> x0, local copies, waits for them, and re-layouts: 41.9 us -> none
    psum x1 -> x0, blocking collectives: 41.5 us -> none  [local(): inner_total = lax.psum(grad_inner_bias, ('seq', 'rows'))]
  transfers between devices with their start and end apart: 11 -> 19, of which waited for: 8 -> 11; matrix products, arithmetic and copies ran while one was open for 7% -> 4% of each run, Pallas kernels for 0% -> 1%
where the time goes in v1:
time: 158 us; the launch traced here: 157 us
  Pallas kernels  59.9 us (38%)
  waiting for transfers between devices  40 us (25%)
  starting transfers between devices  33.8 us (21%)
  local copies, waits for them, and re-layouts  19.1 us (12%)
  other arithmetic  3.16 us (2%)
    ppermute x15, waiting for transfers between devices, exchange(): return lax.ppermute(value, axis, [(i, i ^ bit) for i in range(count)])  35.6 us
    pallas_call x1, Pallas kernels, local(): pl.pallas_call(partial(attend_back_kernel, scale=scale), grid=(PAIRS,), o...  22.6 us
    ppermute x15, starting transfers between devices, exchange(): return lax.ppermute(value, axis, [(i, i ^ bit) for i in range(count)])  22.4 us
    unnamed x60, local copies, waits for them, and re-layouts  14.6 us
    pallas_call x1, Pallas kernels, local(): pl.pallas_call(partial(attend_kernel, scale=scale), grid=(PAIRS,), out_sh...  13.9 us
    pallas_call x1, Pallas kernels, local(): pl.pallas_call(partial(middle_kernel, step=256), out_shape=(shape((tokens...  12.6 us
    ppermute x1, starting transfers between devices, local(): x_low = lax.ppermute(x[block - span:], 'seq', forward)  4.88 us
    ppermute x1, waiting for transfers between devices, local(): x_high = lax.ppermute(x[:span], 'seq', backward)  4.12 us
  transfers between devices with their start and end apart: 19, of which 11 were waited for; matrix products, arithmetic and copies ran while one was open for 4% of the time, Pallas kernels for 1%

profile of v1, /device:TPU:0, one launch (start us, length us, event | category | flops | bytes accessed | tf_op | source)
XLA Modules:
  0.0 157.0 jit_solution(13341972452955853978)
XLA Ops:
  1.7 4.9 %collective-permute-start = (bf16[256,384]{1,0:T(8,128)(2,1)S(1)}, bf16[256,384]{1,0:T(8,128)(2,1)S(1)}, u32[]{:S(2)}, u32[]{:S(2)}) collective-permute-start(bf16[256,384]{1,0:T(8,128)(2,1)S(1)} %get-tuple-element.113), channel_id=1, source_target_pairs={{0,16},{1,17},{2,18},{3,19},{4,20},{5,21},{6,22},{7,23},{8,24},{9,... | collective-permute-start | bytes 589832 | tf_op jit(solution)/shard_map/ppermute | solution.py:546
  6.6 1.3 collective-permute-start.1
  10.7 4.1 %collective-permute-done.1.x_high = bf16[256,384]{1,0:T(8,128)(2,1)S(1)} collective-permute-done((bf16[256,384]{1,0:T(8,128)(2,1)S(1)}, bf16[256,384]{1,0:T(8,128)(2,1)S(1)}, u32[]{:S(2)}, u32[]{:S(2)}) %collective-permute-start.1) | collective-permute-done | bytes 196640 | tf_op jit(solution)/shard_map/ppermute | solution.py:547
  23.3 2.9 %project.1 = (bf16[3,512,128]{2,1,0:T(8,128)(2,1)S(1)}, bf16[3,1024,128]{2,1,0:T(8,128)(2,1)S(1)}, bf16[3,1024,128]{2,1,0:T(8,128)(2,1)S(1)}, bf16[3,512,128]{2,...) custom-call(s32[3]{0:T(128)S(1)} %pad_add_fusion.info, ...), custom_call_target="tpu_custom_call" | custom-call | tf_op jit(solution)/shard_map/project/pallas_call | solution.py:553
  26.2 13.9 %attend.1 = (bf16[512,384]{1,0:T(8,128)(2,1)S(1)}, bf16[3,2,4,128,640]{4,3,2,1,0:T(8,128)(2,1)S(1)}) custom-call(s32[3]{0:T(128)S(1)} %pad_add_fusion.info, bf16[3,512,128]{2,1,0:T(8,128)(2,1)S(1)} %get-tuple-element.55.q, bf16[3,1024,128]{2,1,0:T(8,128)(2,1)S(1)} %get-tuple-element.56.k, bf16[3,1024,128]{2,1,0:T(8,128)(2,1)S(1)} %get-tuple-element.57.v, ...), custom_call_target="tpu_custom_call" | custom-call | tf_op jit(solution)/shard_map/attend/pallas_call | solution.py:594
  40.9 12.6 %middle.1 = (bf16[512,384]{1,0:T(8,128)(2,1)}, f32[512,384]{1,0:T(8,128)}, bf16[512,384]{1,0:T(8,128)(2,1)}, bf16[192,3456]{1,0:T(8,128)(2,1)}, bf16[192,3456]{1...) custom-call(bf16[512,384]{1,0:T(8,128)(2,1)} %bitcast.14, bf16[512,384]{1,0:T(8,128)(2,1)} %copy-done.4, ...), custom_call_target="tpu_custom_call" | custom-call | tf_op jit(solution)/shard_map/middle/pallas_call | solution.py:609
  54.6 22.6 %attend_back.1 = (bf16[512,384]{1,0:T(8,128)(2,1)S(1)}, bf16[1024,384]{1,0:T(8,128)(2,1)S(1)}, bf16[1024,384]{1,0:T(8,128)(2,1)S(1)}, bf16[384,512]{1,0:T(8,128)(2,1)S(1)}, bf16[384,512]{1,0:T(8,128)(2,1)S(1)}) custom-call(bf16[3,512,128]{2,1,0:T(8,128)(2,1)S(1)} %get-tuple-element.55.q, bf16[3,1024,128]{2,1,0:T(8,128)(2,1)S(1)} %get-tuple-element.56.k, ...), custom_call_target="tpu_custom_call" | custom-call | tf_op jit(solution)/shard_map/attend_back/pallas_call | solution.py:645
  77.3 3.9 %weight_grad.1 = (bf16[192,2560]{1,0:T(8,128)(2,1)S(1)}, bf16[192,2560]{1,0:T(8,128)(2,1)S(1)}) custom-call(bf16[512,384]{1,0:T(8,128)(2,1)S(1)} %bitcast.16, bf16[256,384]{1,0:T(8,128)(2,1)S(1)} %collective-permute-done.x_low, bf16[256,384]{1,0:T(8,128)(2,1)S(1)} %collective-permute-done.1.x_high, bf16[512,384]{1,0:T(8,128)(2,1)S(1)} %copy-done.3, ...), custom_call_target="tpu_custom_call" | custom-call | tf_op jit(solution)/shard_map/weight_grad/pallas_call | solution.py:678
  84.1 1.6 collective-permute-start.10
  86.5 1.5 collective-permute-start.15
  88.0 9.5 %collective-permute-done.15 = f32[1,1536]{1,0:T(1,128)S(1)} collective-permute-done((f32[1,1536]{1,0:T(1,128)S(1)}, f32[1,1536]{1,0:T(1,128)S(1)}, u32[]{:S(2)}, u32[]{:S(2)}) %collective-permute-start.15) | collective-permute-done | bytes 6176 | tf_op jit(solution)/shard_map/ppermute | solution.py:44
  97.6 1.6 %collective-permute-start.16 = (f32[1,1536]{1,0:T(1,128)S(1)}, f32[1,1536]{1,0:T(1,128)S(1)}, u32[]{:S(2)}, u32[]{:S(2)}) collective-permute-start(f32[1,1536]{1,0:T(1,128)S(1)} %add.56), channel_id=1, source_target_pairs={{0,4},{1,5},{2,6},{3,7},{4,0},{5,1},{6,2},{7,3},{8,12},{9,13},{10,... | collective-permute-start | bytes 18440 | tf_op jit(solution)/shard_map/ppermute | solution.py:44
  99.2 2.1 %collective-permute-done.16 = f32[1,1536]{1,0:T(1,128)S(1)} collective-permute-done((f32[1,1536]{1,0:T(1,128)S(1)}, f32[1,1536]{1,0:T(1,128)S(1)}, u32[]{:S(2)}, u32[]{:S(2)}) %collective-permute-start.16) | collective-permute-done | bytes 6176 | tf_op jit(solution)/shard_map/ppermute | solution.py:44
  101.3 2.6 %collective-permute-start.17 = (f32[1,1536]{1,0:T(1,128)S(1)}, f32[1,1536]{1,0:T(1,128)S(1)}, u32[]{:S(2)}, u32[]{:S(2)}) collective-permute-start(f32[1,1536]{1,0:T(1,128)S(1)} %add.57), channel_id=1, source_target_pairs={{0,8},{1,9},{2,10},{3,11},{4,12},{5,13},{6,14},{7,15},{8,0},{9,1},... | collective-permute-start | bytes 18440 | tf_op jit(solution)/shard_map/ppermute | solution.py:44
  103.9 1.9 %collective-permute-done.17 = f32[1,1536]{1,0:T(1,128)S(1)} collective-permute-done((f32[1,1536]{1,0:T(1,128)S(1)}, f32[1,1536]{1,0:T(1,128)S(1)}, u32[]{:S(2)}, u32[]{:S(2)}) %collective-permute-start.17) | collective-permute-done | bytes 6176 | tf_op jit(solution)/shard_map/ppermute | solution.py:44
  106.0 1.4 input_grad.1
  107.4 3.9 %collective-permute-start.2 = (bf16[256,384]{1,0:T(8,128)(2,1)S(1)}, bf16[256,384]{1,0:T(8,128)(2,1)S(1)}, u32[]{:S(2)}, u32[]{:S(2)}) collective-permute-start(bf16[256,384]{1,0:T(8,128)(2,1)S(1)} %get-tuple-element.71), channel_id=1, source_target_pairs={{0,16},{1,17},{2,18},{3,19},{4,20},{5,21},{6,22},{7,23},{8,24},{9,... | collective-permute-start | bytes 589832 | tf_op jit(solution)/shard_map/ppermute | solution.py:699
  111.3 1.3 collective-permute-start.3
  113.6 1.6 collective-permute-start.5
  115.3 1.6 %collective-permute-start.11 = (bf16[48,2560]{1,0:T(8,128)(2,1)S(1)}, bf16[48,2560]{1,0:T(8,128)(2,1)S(1)}, u32[]{:S(2)}, u32[]{:S(2)}) collective-permute-start(bf16[48,2560]{1,0:T(8,128)(2,1)S(1)} %slice.85), channel_id=1, source_target_pairs={{0,4},{1,5},{2,6},{3,7},{4,0},{5,1},{6,2},{7,3},{8,12},{9,13},{10,... | collective-permute-start | bytes 737288 | tf_op jit(solution)/shard_map/ppermute | solution.py:44
  116.9 10.0 %collective-permute-done.5 = bf16[96,3456]{1,0:T(8,128)(2,1)S(1)} collective-permute-done((bf16[96,3456]{1,0:T(8,128)(2,1)S(1)}, bf16[96,3456]{1,0:T(8,128)(2,1)S(1)}, u32[]{:S(2)}, u32[]{:S(2)}) %collective-permute-start.5) | collective-permute-done | bytes 663584 | tf_op jit(solution)/shard_map/ppermute | solution.py:44
  127.1 1.6 %collective-permute-start.6 = (bf16[48,3456]{1,0:T(8,128)(2,1)S(1)}, bf16[48,3456]{1,0:T(8,128)(2,1)S(1)}, u32[]{:S(2)}, u32[]{:S(2)}) collective-permute-start(bf16[48,3456]{1,0:T(8,128)(2,1)S(1)} %slice.79), channel_id=1, source_target_pairs={{0,4},{1,5},{2,6},{3,7},{4,0},{5,1},{6,2},{7,3},{8,12},{9,13},{10,... | collective-permute-start | bytes 995336 | tf_op jit(solution)/shard_map/ppermute | solution.py:44
  128.8 2.6 %collective-permute-start.12 = (bf16[24,2560]{1,0:T(8,128)(2,1)S(1)}, bf16[24,2560]{1,0:T(8,128)(2,1)S(1)}, u32[]{:S(2)}, u32[]{:S(2)}) collective-permute-start(bf16[24,2560]{1,0:T(8,128)(2,1)S(1)} %slice.87), channel_id=1, source_target_pairs={{0,8},{1,9},{2,10},{3,11},{4,12},{5,13},{6,14},{7,15},{8,0},{9,1},... | collective-permute-start | bytes 368648 | tf_op jit(solution)/shard_map/ppermute | solution.py:44
  131.4 5.0 %collective-permute-done.6 = bf16[48,3456]{1,0:T(8,128)(2,1)S(1)} collective-permute-done((bf16[48,3456]{1,0:T(8,128)(2,1)S(1)}, bf16[48,3456]{1,0:T(8,128)(2,1)S(1)}, u32[]{:S(2)}, u32[]{:S(2)}) %collective-permute-start.6) | collective-permute-done | bytes 331808 | tf_op jit(solution)/shard_map/ppermute | solution.py:44
  136.5 2.2 %collective-permute-start.7 = (bf16[24,3456]{1,0:T(8,128)(2,1)S(1)}, bf16[24,3456]{1,0:T(8,128)(2,1)S(1)}, u32[]{:S(2)}, u32[]{:S(2)}) collective-permute-start(bf16[24,3456]{1,0:T(8,128)(2,1)S(1)} %slice.81), channel_id=1, source_target_pairs={{0,8},{1,9},{2,10},{3,11},{4,12},{5,13},{6,14},{7,15},{8,0},{9,1},... | collective-permute-start | bytes 497672 | tf_op jit(solution)/shard_map/ppermute | solution.py:44
  138.7 2.5 %collective-permute-start.13 = (bf16[24,2560]{1,0:T(8,128)(2,1)S(1)}, bf16[24,2560]{1,0:T(8,128)(2,1)S(1)}, u32[]{:S(2)}, u32[]{:S(2)}) collective-permute-start(bf16[24,2560]{1,0:T(8,128)(2,1)S(1)} %slice_add_fusion.5.rest), channel_id=1, source_target_pairs={{0,16},{16,0},{1,17},{17,1},{2,18},{18,2},{3,19},{19,3},{4,20},{20... | collective-permute-start | bytes 368648 | tf_op jit(solution)/shard_map/ppermute | solution.py:44
  141.2 3.3 %collective-permute-done.7 = bf16[24,3456]{1,0:T(8,128)(2,1)S(1)} collective-permute-done((bf16[24,3456]{1,0:T(8,128)(2,1)S(1)}, bf16[24,3456]{1,0:T(8,128)(2,1)S(1)}, u32[]{:S(2)}, u32[]{:S(2)}) %collective-permute-start.7) | collective-permute-done | bytes 165920 | tf_op jit(solution)/shard_map/ppermute | solution.py:44
  144.6 2.2 %collective-permute-start.8 = (bf16[24,3456]{1,0:T(8,128)(2,1)S(1)}, bf16[24,3456]{1,0:T(8,128)(2,1)S(1)}, u32[]{:S(2)}, u32[]{:S(2)}) collective-permute-start(bf16[24,3456]{1,0:T(8,128)(2,1)S(1)} %slice_add_fusion.4.mid), channel_id=1, source_target_pairs={{0,16},{16,0},{1,17},{17,1},{2,18},{18,2},{3,19},{19,3},{4,20},{20... | collective-permute-start | bytes 497672 | tf_op jit(solution)/shard_map/ppermute | solution.py:44
  147.6 2.4 %collective-permute-done.8.mid_other = bf16[24,3456]{1,0:T(8,128)(2,1)S(1)} collective-permute-done((bf16[24,3456]{1,0:T(8,128)(2,1)S(1)}, bf16[24,3456]{1,0:T(8,128)(2,1)S(1)}, u32[]{:S(2)}, u32[]{:S(2)}) %collective-permute-start.8) | collective-permute-done | bytes 165920 | tf_op jit(solution)/shard_map/ppermute | solution.py:44
  150.8 2.5 %final.1 = (f32[24,384]{1,0:T(8,128)}, f32[24,384]{1,0:T(8,128)}, f32[24,384]{1,0:T(8,128)}, f32[24,384]{1,0:T(8,128)}, f32[512,24]{1,0:T(8,128)}, /*index=5*/f3...) custom-call(bf16[24,3456]{1,0:T(8,128)(2,1)} %copy-done.24, ...), custom_call_target="tpu_custom_call" | custom-call | tf_op jit(solution)/shard_map/final/pallas_call | solution.py:730
  153.2 2.0 %copy.35 = f32[1536,24]{0,1:T(8,128)} copy(f32[1536,24]{1,0:T(8,128)} %get-tuple-element.108) | data formatting | bytes 294912
  155.3 1.7 %copy.34 = f32[512,24]{0,1:T(8,128)} copy(f32[512,24]{1,0:T(8,128)} %get-tuple-element.100) | data formatting | bytes 98304
  (99 shorter events, 20.8 us)
Async XLA Ops:
  1.7 9.0 %collective-permute-start = (bf16[256,384]{1,0:T(8,128)(2,1)S(1)}, bf16[256,384]{1,0:T(8,128)(2,1)S(1)}, u32[]{:S(2)}, u32[]{:S(2)}) collective-permute-start(bf16[256,384]{1,0:T(8,128)(2,1)S(1)} %get-tuple-element.113), channel_id=1, source_target_pairs={{0,16},{1,17},{2,18},{3,19},{4,20},{5,21},{6,22},{7,23},{8,24},{9,... | collective-permute-start | bytes 589832 | tf_op jit(solution)/shard_map/ppermute | solution.py:546
  6.6 8.3 %collective-permute-start.1 = (bf16[256,384]{1,0:T(8,128)(2,1)S(1)}, bf16[256,384]{1,0:T(8,128)(2,1)S(1)}, u32[]{:S(2)}, u32[]{:S(2)}) collective-permute-start(bf16[256,384]{1,0:T(8,128)(2,1)S(1)} %get-tuple-element.112), channel_id=1, source_target_pairs={{16,0},{17,1},{18,2},{19,3},{20,4},{21,5},{22,6},{23,7},{24,8},{25... | collective-permute-start | bytes 589832 | tf_op jit(solution)/shard_map/ppermute | solution.py:547
  26.2 13.9 %copy-start.16 = (bf16[384,384]{1,0:T(8,128)(2,1)}, bf16[384,384]{1,0:T(8,128)(2,1)S(1)}, u32[]{:S(2)}) copy-start(bf16[384,384]{1,0:T(8,128)(2,1)S(1)} %get-tuple-element.61.order) | copy-start | bytes 884740
  40.9 12.6 %copy-start.5 = (bf16[512,384]{1,0:T(8,128)(2,1)S(1)}, bf16[512,384]{1,0:T(8,128)(2,1)}, u32[]{:S(2)}) copy-start(bf16[512,384]{1,0:T(8,128)(2,1)} %copy-done.4) | copy-start | bytes 1179652
  54.5 22.7 %copy-start.1 = (bf16[1,512,384]{2,1,0:T(8,128)(2,1)S(1)}, bf16[1,512,384]{2,1,0:T(8,128)(2,1)}, u32[]{:S(2)}) copy-start(bf16[1,512,384]{2,1,0:T(8,128)(2,1)} %param.18) | copy-start | bytes 1179652
  54.5 22.7 %copy-start.3 = (bf16[512,384]{1,0:T(8,128)(2,1)S(1)}, bf16[512,384]{1,0:T(8,128)(2,1)}, u32[]{:S(2)}) copy-start(bf16[512,384]{1,0:T(8,128)(2,1)} %rel.3) | copy-start | bytes 1179652
  54.5 22.7 %copy-start.7 = (bf16[384,384]{1,0:T(8,128)(2,1)S(1)}, bf16[384,384]{1,0:T(8,128)(2,1)}, u32[]{:S(2)}) copy-start(bf16[384,384]{1,0:T(8,128)(2,1)} %w_pos_key.3) | copy-start | bytes 884740
  54.5 22.7 %copy-start.9 = (bf16[384,384]{1,0:T(8,128)(2,1)S(1)}, bf16[384,384]{1,0:T(8,128)(2,1)}, u32[]{:S(2)}) copy-start(bf16[384,384]{1,0:T(8,128)(2,1)} %w_pos_query.3) | copy-start | bytes 884740
  54.6 22.7 %copy-start.17 = (bf16[384,384]{1,0:T(8,128)(2,1)S(1)}, bf16[384,384]{1,0:T(8,128)(2,1)}, u32[]{:S(2)}) copy-start(bf16[384,384]{1,0:T(8,128)(2,1)} %copy-done.16) | copy-start | bytes 884740
  54.6 22.7 %copy-start.21 = (f32[16,384]{1,0:T(8,128)S(1)}, f32[16,384]{1,0:T(8,128)}, u32[]{:S(2)}) copy-start(f32[16,384]{1,0:T(8,128)} %get-tuple-element.77.rows) | copy-start | bytes 73732
  81.2 2.6 %collective-permute-start.9 = (bf16[192,2560]{1,0:T(8,128)(2,1)S(1)}, bf16[192,2560]{1,0:T(8,128)(2,1)S(1)}, u32[]{:S(2)}, u32[]{:S(2)}) collective-permute-start(bf16[192,2560]{1,0:T(8,128)(2,1)S(1)} %get-tuple-element.79), channel_id=1, source_target_pairs={{0,1},{1,0},{2,3},{3,2},{4,5},{5,4},{6,7},{7,6},{8,9},{9,8},{10,11... | collective-permute-start | bytes 2949128 | tf_op jit(solution)/shard_map/ppermute | solution.py:44
  81.3 32.0 %collective-permute-start.4 = (bf16[192,3456]{1,0:T(8,128)(2,1)S(1)}, bf16[192,3456]{1,0:T(8,128)(2,1)S(1)}, u32[]{:S(2)}, u32[]{:S(2)}) collective-permute-start(bf16[192,3456]{1,0:T(8,128)(2,1)S(1)} %copy-done.28), channel_id=1, source_target_pairs={{0,1},{1,0},{2,3},{3,2},{4,5},{5,4},{6,7},{7,6},{8,9},{9,8},{10,11... | collective-permute-start | bytes 3981320 | tf_op jit(solution)/shard_map/ppermute | solution.py:44
  82.6 3.2 %collective-permute-start.14 = (f32[1,1536]{1,0:T(1,128)S(1)}, f32[1,1536]{1,0:T(1,128)S(1)}, u32[]{:S(2)}, u32[]{:S(2)}) collective-permute-start(f32[1,1536]{1,0:T(1,128)S(1)} %slice.75), channel_id=1, source_target_pairs={{0,1},{1,0},{2,3},{3,2},{4,5},{5,4},{6,7},{7,6},{8,9},{9,8},{10,11... | collective-permute-start | bytes 18440 | tf_op jit(solution)/shard_map/ppermute | solution.py:44
  83.8 22.1 %copy-start.11 = (bf16[384,384]{1,0:T(8,128)(2,1)S(1)}, bf16[384,384]{1,0:T(8,128)(2,1)}, u32[]{:S(2)}) copy-start(bf16[384,384]{1,0:T(8,128)(2,1)} %w_query.3) | copy-start | bytes 884740
  83.8 22.2 %copy-start.13 = (bf16[384,384]{1,0:T(8,128)(2,1)S(1)}, bf16[384,384]{1,0:T(8,128)(2,1)}, u32[]{:S(2)}) copy-start(bf16[384,384]{1,0:T(8,128)(2,1)} %w_key.3) | copy-start | bytes 884740
  83.8 22.2 %copy-start.15 = (bf16[384,384]{1,0:T(8,128)(2,1)S(1)}, bf16[384,384]{1,0:T(8,128)(2,1)}, u32[]{:S(2)}) copy-start(bf16[384,384]{1,0:T(8,128)(2,1)} %w_value.3) | copy-start | bytes 884740
  83.8 22.2 %copy-start.18 = (f32[512,384]{1,0:T(8,128)S(1)}, f32[512,384]{1,0:T(8,128)}, u32[]{:S(2)}) copy-start(f32[512,384]{1,0:T(8,128)} %get-tuple-element.69.d_first) | copy-start | bytes 2359300
  84.1 31.1 %collective-permute-start.10 = (bf16[96,2560]{1,0:T(8,128)(2,1)S(1)}, bf16[96,2560]{1,0:T(8,128)(2,1)S(1)}, u32[]{:S(2)}, u32[]{:S(2)}) collective-permute-start(bf16[96,2560]{1,0:T(8,128)(2,1)S(1)} %slice.83), channel_id=1, source_target_pairs={{0,2},{1,3},{2,0},{3,1},{4,6},{5,7},{6,4},{7,5},{8,10},{9,11},{10,... | collective-permute-start | bytes 1474568 | tf_op jit(solution)/shard_map/ppermute | solution.py:44
  86.5 11.0 %collective-permute-start.15 = (f32[1,1536]{1,0:T(1,128)S(1)}, f32[1,1536]{1,0:T(1,128)S(1)}, u32[]{:S(2)}, u32[]{:S(2)}) collective-permute-start(f32[1,1536]{1,0:T(1,128)S(1)} %slice_add_fusion.6), channel_id=1, source_target_pairs={{0,2},{1,3},{2,0},{3,1},{4,6},{5,7},{6,4},{7,5},{8,10},{9,11},{10,... | collective-permute-start | bytes 18440 | tf_op jit(solution)/shard_map/ppermute | solution.py:44
  97.6 3.7 %collective-permute-start.16 = (f32[1,1536]{1,0:T(1,128)S(1)}, f32[1,1536]{1,0:T(1,128)S(1)}, u32[]{:S(2)}, u32[]{:S(2)}) collective-permute-start(f32[1,1536]{1,0:T(1,128)S(1)} %add.56), channel_id=1, source_target_pairs={{0,4},{1,5},{2,6},{3,7},{4,0},{5,1},{6,2},{7,3},{8,12},{9,13},{10,... | collective-permute-start | bytes 18440 | tf_op jit(solution)/shard_map/ppermute | solution.py:44
  101.3 4.6 %collective-permute-start.17 = (f32[1,1536]{1,0:T(1,128)S(1)}, f32[1,1536]{1,0:T(1,128)S(1)}, u32[]{:S(2)}, u32[]{:S(2)}) collective-permute-start(f32[1,1536]{1,0:T(1,128)S(1)} %add.57), channel_id=1, source_target_pairs={{0,8},{1,9},{2,10},{3,11},{4,12},{5,13},{6,14},{7,15},{8,0},{9,1},... | collective-permute-start | bytes 18440 | tf_op jit(solution)/shard_map/ppermute | solution.py:44
  105.9 6.7 %collective-permute-start.18 = (f32[1,1536]{1,0:T(1,128)S(1)}, f32[1,1536]{1,0:T(1,128)S(1)}, u32[]{:S(2)}, u32[]{:S(2)}) collective-permute-start(f32[1,1536]{1,0:T(1,128)S(1)} %add.58), channel_id=1, source_target_pairs={{0,16},{16,0},{1,17},{17,1},{2,18},{18,2},{3,19},{19,3},{4,20},{20... | collective-permute-start | bytes 18440 | tf_op jit(solution)/shard_map/ppermute | solution.py:44
  107.4 39.4 %collective-permute-start.2 = (bf16[256,384]{1,0:T(8,128)(2,1)S(1)}, bf16[256,384]{1,0:T(8,128)(2,1)S(1)}, u32[]{:S(2)}, u32[]{:S(2)}) collective-permute-start(bf16[256,384]{1,0:T(8,128)(2,1)S(1)} %get-tuple-element.71), channel_id=1, source_target_pairs={{0,16},{1,17},{2,18},{3,19},{4,20},{5,21},{6,22},{7,23},{8,24},{9,... | collective-permute-start | bytes 589832 | tf_op jit(solution)/shard_map/ppermute | solution.py:699
  111.3 35.4 %collective-permute-start.3 = (bf16[256,384]{1,0:T(8,128)(2,1)S(1)}, bf16[256,384]{1,0:T(8,128)(2,1)S(1)}, u32[]{:S(2)}, u32[]{:S(2)}) collective-permute-start(bf16[256,384]{1,0:T(8,128)(2,1)S(1)} %get-tuple-element.72), channel_id=1, source_target_pairs={{16,0},{17,1},{18,2},{19,3},{20,4},{21,5},{22,6},{23,7},{24,8},{25... | collective-permute-start | bytes 589832 | tf_op jit(solution)/shard_map/ppermute | solution.py:698
  113.6 13.3 %collective-permute-start.5 = (bf16[96,3456]{1,0:T(8,128)(2,1)S(1)}, bf16[96,3456]{1,0:T(8,128)(2,1)S(1)}, u32[]{:S(2)}, u32[]{:S(2)}) collective-permute-start(bf16[96,3456]{1,0:T(8,128)(2,1)S(1)} %slice.77), channel_id=1, source_target_pairs={{0,2},{1,3},{2,0},{3,1},{4,6},{5,7},{6,4},{7,5},{8,10},{9,11},{10,... | collective-permute-start | bytes 1990664 | tf_op jit(solution)/shard_map/ppermute | solution.py:44
  115.3 13.4 %collective-permute-start.11 = (bf16[48,2560]{1,0:T(8,128)(2,1)S(1)}, bf16[48,2560]{1,0:T(8,128)(2,1)S(1)}, u32[]{:S(2)}, u32[]{:S(2)}) collective-permute-start(bf16[48,2560]{1,0:T(8,128)(2,1)S(1)} %slice.85), channel_id=1, source_target_pairs={{0,4},{1,5},{2,6},{3,7},{4,0},{5,1},{6,2},{7,3},{8,12},{9,13},{10,... | collective-permute-start | bytes 737288 | tf_op jit(solution)/shard_map/ppermute | solution.py:44
  127.1 9.3 %collective-permute-start.6 = (bf16[48,3456]{1,0:T(8,128)(2,1)S(1)}, bf16[48,3456]{1,0:T(8,128)(2,1)S(1)}, u32[]{:S(2)}, u32[]{:S(2)}) collective-permute-start(bf16[48,3456]{1,0:T(8,128)(2,1)S(1)} %slice.79), channel_id=1, source_target_pairs={{0,4},{1,5},{2,6},{3,7},{4,0},{5,1},{6,2},{7,3},{8,12},{9,13},{10,... | collective-permute-start | bytes 995336 | tf_op jit(solution)/shard_map/ppermute | solution.py:44
  128.8 9.9 %collective-permute-start.12 = (bf16[24,2560]{1,0:T(8,128)(2,1)S(1)}, bf16[24,2560]{1,0:T(8,128)(2,1)S(1)}, u32[]{:S(2)}, u32[]{:S(2)}) collective-permute-start(bf16[24,2560]{1,0:T(8,128)(2,1)S(1)} %slice.87), channel_id=1, source_target_pairs={{0,8},{1,9},{2,10},{3,11},{4,12},{5,13},{6,14},{7,15},{8,0},{9,1},... | collective-permute-start | bytes 368648 | tf_op jit(solution)/shard_map/ppermute | solution.py:44
  136.5 8.1 %collective-permute-start.7 = (bf16[24,3456]{1,0:T(8,128)(2,1)S(1)}, bf16[24,3456]{1,0:T(8,128)(2,1)S(1)}, u32[]{:S(2)}, u32[]{:S(2)}) collective-permute-start(bf16[24,3456]{1,0:T(8,128)(2,1)S(1)} %slice.81), channel_id=1, source_target_pairs={{0,8},{1,9},{2,10},{3,11},{4,12},{5,13},{6,14},{7,15},{8,0},{9,1},... | collective-permute-start | bytes 497672 | tf_op jit(solution)/shard_map/ppermute | solution.py:44
  138.7 9.0 %copy-start.25 = (bf16[24,2560]{1,0:T(8,128)(2,1)}, bf16[24,2560]{1,0:T(8,128)(2,1)S(1)}, u32[]{:S(2)}) copy-start(bf16[24,2560]{1,0:T(8,128)(2,1)S(1)} %slice_add_fusion.5.rest) | copy-start | bytes 368644
  138.7 9.0 %collective-permute-start.13 = (bf16[24,2560]{1,0:T(8,128)(2,1)S(1)}, bf16[24,2560]{1,0:T(8,128)(2,1)S(1)}, u32[]{:S(2)}, u32[]{:S(2)}) collective-permute-start(bf16[24,2560]{1,0:T(8,128)(2,1)S(1)} %slice_add_fusion.5.rest), channel_id=1, source_target_pairs={{0,16},{16,0},{1,17},{17,1},{2,18},{18,2},{3,19},{19,3},{4,20},{20... | collective-permute-start | bytes 368648 | tf_op jit(solution)/shard_map/ppermute | solution.py:44
  144.6 5.5 %collective-permute-start.8 = (bf16[24,3456]{1,0:T(8,128)(2,1)S(1)}, bf16[24,3456]{1,0:T(8,128)(2,1)S(1)}, u32[]{:S(2)}, u32[]{:S(2)}) collective-permute-start(bf16[24,3456]{1,0:T(8,128)(2,1)S(1)} %slice_add_fusion.4.mid), channel_id=1, source_target_pairs={{0,16},{16,0},{1,17},{17,1},{2,18},{18,2},{3,19},{19,3},{4,20},{20... | collective-permute-start | bytes 497672 | tf_op jit(solution)/shard_map/ppermute | solution.py:44
  (16 other events, 30.0 us)
